TPU v7x, 32 devices: a whole 2x2x4 slice. The times are simulated.
32 devices in a mesh: shard: 2 (over core), ctx: 4 (over y, x), tensor: 4 (over z).
Axes of the slice: x: 2, y: 2, z: 4, core: 2. Of those that a mesh axis runs over, the one named last changes fastest.
Arguments:
- inputs: bfloat16 [2, 2048, 2048], P('shard', ('ctx', 'tensor')), may hold values from -6 to 6
- out_grad: bfloat16 [2, 2048, 2048], P('shard', ('ctx', 'tensor')), may hold values from -6 to 6
- block_order: int32 [2, 8], P('shard'), may hold values from 0 to 7, each once within a row
- gain_attn: bfloat16 [2048], P(('shard', 'ctx')), may hold values from 0.5 to 1.5
- w_query: bfloat16 [2048, 2048], P(('shard', 'ctx'), 'tensor'), may hold values from -0.125 to 0.125
- w_keyval: bfloat16 [2048, 512], P(('shard', 'ctx'), 'tensor'), may hold values from -0.125 to 0.125
- w_output: bfloat16 [2048, 2048], P(('shard', 'ctx'), 'tensor'), may hold values from -3 to 3
- gain_mlp: bfloat16 [2048], P(('shard', 'ctx')), may hold values from 0.5 to 1.5
- w_gate: bfloat16 [2048, 5632], P(('shard', 'ctx'), 'tensor'), may hold values from -0.125 to 0.125
- w_up: bfloat16 [2048, 5632], P(('shard', 'ctx'), 'tensor'), may hold values from -0.125 to 0.125
- w_down: bfloat16 [2048, 5632], P(('shard', 'ctx'), 'tensor'), may hold values from -0.078125 to 0.078125
Outputs:
- layer_out: bfloat16 [2, 2048, 2048], P('shard', ('ctx', 'tensor'))
- input_grad: float32 [2, 2048, 2048], P('shard', ('ctx', 'tensor'))
- grad_gain_attn: float32 [2048], P(('shard', 'ctx'))
- grad_query: float32 [2048, 2048], P(('shard', 'ctx'), 'tensor')
- grad_keyval: float32 [2048, 512], P(('shard', 'ctx'), 'tensor')
- grad_output: float32 [2048, 2048], P(('shard', 'ctx'), 'tensor')
- grad_gain_mlp: float32 [2048], P(('shard', 'ctx'))
- grad_gate: float32 [2048, 5632], P(('shard', 'ctx'), 'tensor')
- grad_up: float32 [2048, 5632], P(('shard', 'ctx'), 'tensor')
- grad_down: float32 [2048, 5632], P(('shard', 'ctx'), 'tensor')
Inputs may be any that keep to these rules, and one draw needn't show every extreme that they name: `block_order`: each row is a permutation of the blocks of one sequence.
All inputs are finite; a program needn't handle non-finite values.
Results may differ from a plain program's by a relative error of at most 0.014.
Values may be sent and summed in bfloat16 or wider, within the bound.
A program may use at most 192 MiB of HBM per device.

v0:
```python
import jax
import jax.numpy as jnp
from jax import lax
from jax.sharding import PartitionSpec as P

HD = 64
BLOCK = 256
BLOCKS = 8
epsilon = 1e-05
blocked = -1e30


def apply_norm(values_in):
    inverse_root_mean = lax.rsqrt(jnp.mean(values_in * values_in, -1, keepdims=True) + epsilon)
    return (values_in * inverse_root_mean, inverse_root_mean)


def norm_backward_pass(normed_gradient, unit_rows, inverse_root_mean, norm_scale):
    unit_rows_gradient = normed_gradient * norm_scale
    scale_gradient = jnp.sum(normed_gradient * unit_rows, axis=(0, 1))
    value_gradients = inverse_root_mean * (
        unit_rows_gradient - unit_rows * jnp.mean(unit_rows_gradient * unit_rows, -1, keepdims=True)
    )
    return (scale_gradient, value_gradients)


def rotary_tables(position, width):
    half_width = width // 2
    frequency = 10000.0 ** (-jnp.arange(half_width, dtype=jnp.float32) * 2.0 / width)
    angles = position.astype(jnp.float32)[..., None] * frequency
    return (jnp.cos(angles)[:, :, None, :], jnp.sin(angles)[:, :, None, :])


def rotate(values_in, cosine_table, sine_table):
    half_width = values_in.shape[-1] // 2
    first_half = values_in[..., :half_width]
    second = values_in[..., half_width:]
    return jnp.concatenate(
        [
            first_half * cosine_table - second * sine_table,
            second * cosine_table + first_half * sine_table,
        ],
        -1,
    )


def unrotate(grad_in, cosine_table, sine_table):
    half_width = grad_in.shape[-1] // 2
    first_half = grad_in[..., :half_width]
    second = grad_in[..., half_width:]
    return jnp.concatenate(
        [
            first_half * cosine_table + second * sine_table,
            second * cosine_table - first_half * sine_table,
        ],
        -1,
    )


def broadcast_rows(values_in):
    return lax.all_gather(values_in, "tensor", axis=1, tiled=True)


def spread_grads(values_in):
    return lax.all_gather(values_in, "tensor", axis=1, tiled=True)


def branch_sum(partial_sum):
    return lax.psum_scatter(partial_sum, "tensor", scatter_dimension=1, tiled=True)


def input_sum(partial_sum):
    return lax.psum_scatter(partial_sum, "tensor", scatter_dimension=1, tiled=True)


def body(
    inputs,
    out_grad,
    block_order,
    gain_attn,
    w_query,
    w_keyval,
    w_output,
    gain_mlp,
    w_gate,
    w_up,
    w_down,
):
    seq_count = inputs.shape[0]
    length = BLOCK * BLOCKS
    query_rows = length // lax.axis_size("ctx")
    heads_here = w_query.shape[1] // HD
    groups_here = w_keyval.shape[1] // (2 * HD)
    per_group = heads_here // groups_here
    inv_root = HD ** (-0.5)
    f32 = jnp.float32
    brain_float_sixteen = jnp.bfloat16
    slot_index = jnp.arange(length, dtype=jnp.int32)
    chooser = (slot_index // BLOCK)[:, None] == jnp.arange(BLOCKS, dtype=jnp.int32)[None, :]
    block_all = jnp.sum(jnp.where(chooser[None, :, :], block_order[:, None, :], 0), axis=-1)
    position_all = block_all * BLOCK + slot_index % BLOCK
    row_start = lax.axis_index("ctx") * query_rows
    block_here = lax.dynamic_slice_in_dim(block_all, row_start, query_rows, 1)
    position_here = lax.dynamic_slice_in_dim(position_all, row_start, query_rows, 1)
    allowed = block_all[:, None, :] <= block_here[:, :, None]
    cosine_table, sine_table = rotary_tables(position_here, HD)
    group_ids = jnp.arange(heads_here, dtype=jnp.int32) // per_group
    attention_norm_scale, query_all, keyval_all, output_all = (
        lax.all_gather(gain_attn, ("shard", "ctx"), axis=0, tiled=True),
        lax.all_gather(w_query, ("shard", "ctx"), axis=0, tiled=True),
        lax.all_gather(w_keyval, ("shard", "ctx"), axis=0, tiled=True),
        lax.all_gather(w_output, ("shard", "ctx"), axis=0, tiled=True),
    )
    feedforward_norm_scale, gate_all, up_all, down_all = (
        lax.all_gather(gain_mlp, ("shard", "ctx"), axis=0, tiled=True),
        lax.all_gather(w_gate, ("shard", "ctx"), axis=0, tiled=True),
        lax.all_gather(w_up, ("shard", "ctx"), axis=0, tiled=True),
        lax.all_gather(w_down, ("shard", "ctx"), axis=0, tiled=True),
    )
    attention_norm_scale = attention_norm_scale.astype(f32)
    feedforward_norm_scale = feedforward_norm_scale.astype(f32)
    residual_stream = inputs.astype(f32)
    first_unit_rows, first_inverse_root = apply_norm(residual_stream)
    first_normed = broadcast_rows(
        (first_unit_rows * attention_norm_scale).astype(brain_float_sixteen)
    )
    query_raw = jnp.einsum("sqd,dh->sqh", first_normed, query_all, preferred_element_type=f32)
    keyval_raw = jnp.einsum("sqd,dh->sqh", first_normed, keyval_all, preferred_element_type=f32)
    query_raw = query_raw.reshape(seq_count, query_rows, heads_here, HD)
    keyval_raw = keyval_raw.reshape(seq_count, query_rows, groups_here, 2 * HD)
    queries = rotate(query_raw, cosine_table, sine_table).astype(brain_float_sixteen)
    keys_here = rotate(keyval_raw[..., :HD], cosine_table, sine_table).astype(brain_float_sixteen)
    values_here = keyval_raw[..., HD:].astype(brain_float_sixteen)
    keyval_here = jnp.concatenate([keys_here, values_here], -1).reshape(
        seq_count, query_rows, groups_here * 2 * HD
    )
    keyval_seq = lax.all_gather(keyval_here, "ctx", axis=1, tiled=True).reshape(
        seq_count, length, groups_here, 2 * HD
    )
    query_heads = jnp.moveaxis(queries, 2, 0)

    def scores_of(query_head, group_id):
        keyval_group = lax.dynamic_index_in_dim(keyval_seq, group_id, 2, keepdims=False)
        keys_group = keyval_group[..., :HD]
        values_group = keyval_group[..., HD:]
        raw_scores = (
            jnp.einsum("sqd,skd->sqk", query_head, keys_group, preferred_element_type=f32)
            * inv_root
        )
        return (jnp.where(allowed, raw_scores, blocked), keys_group, values_group)

    def forward_head(operands):
        query_head, group_id = operands
        masked, keys_group, values_group = scores_of(query_head, group_id)
        row_max = jnp.max(masked, -1, keepdims=True)
        exponent = jnp.exp(masked - row_max)
        expsum = jnp.sum(exponent, -1, keepdims=True)
        weights = (exponent / expsum).astype(brain_float_sixteen)
        head_out = jnp.einsum(
            "sqk,skd->sqd", weights, values_group, preferred_element_type=f32
        ).astype(brain_float_sixteen)
        return (head_out, (row_max + jnp.log(expsum))[..., 0])

    head_outs, log_sums = lax.map(forward_head, (query_heads, group_ids))
    attn_out = jnp.moveaxis(head_outs, 0, 2).reshape(seq_count, query_rows, heads_here * HD)
    attn_branch = branch_sum(
        jnp.einsum("sqh,dh->sqd", attn_out, output_all, preferred_element_type=f32)
    )
    between_rows = residual_stream + attn_branch
    second_unit_rows, second_inverse_root = apply_norm(between_rows)
    second_normed = broadcast_rows(
        (second_unit_rows * feedforward_norm_scale).astype(brain_float_sixteen)
    )
    gate_act = jnp.einsum("sqd,df->sqf", second_normed, gate_all, preferred_element_type=f32)
    up_act = jnp.einsum("sqd,df->sqf", second_normed, up_all, preferred_element_type=f32)
    sig_gate = jax.nn.sigmoid(gate_act)
    silu_gate = gate_act * sig_gate
    hidden = (silu_gate * up_act).astype(brain_float_sixteen)
    mlp_branch = branch_sum(jnp.einsum("sqf,df->sqd", hidden, down_all, preferred_element_type=f32))
    layer_out = (between_rows + mlp_branch).astype(brain_float_sixteen)
    attention_norm_scale, query_all, keyval_all, output_all = (
        lax.all_gather(gain_attn, ("shard", "ctx"), axis=0, tiled=True),
        lax.all_gather(w_query, ("shard", "ctx"), axis=0, tiled=True),
        lax.all_gather(w_keyval, ("shard", "ctx"), axis=0, tiled=True),
        lax.all_gather(w_output, ("shard", "ctx"), axis=0, tiled=True),
    )
    feedforward_norm_scale, gate_all, up_all, down_all = (
        lax.all_gather(gain_mlp, ("shard", "ctx"), axis=0, tiled=True),
        lax.all_gather(w_gate, ("shard", "ctx"), axis=0, tiled=True),
        lax.all_gather(w_up, ("shard", "ctx"), axis=0, tiled=True),
        lax.all_gather(w_down, ("shard", "ctx"), axis=0, tiled=True),
    )
    attention_norm_scale = attention_norm_scale.astype(f32)
    feedforward_norm_scale = feedforward_norm_scale.astype(f32)
    grad_mlp_rows = spread_grads(out_grad)
    d_hidden = jnp.einsum("sqd,df->sqf", grad_mlp_rows, down_all, preferred_element_type=f32)
    grad_down_w = jnp.einsum("sqd,sqf->df", grad_mlp_rows, hidden, preferred_element_type=f32)
    d_gate = (d_hidden * up_act * sig_gate * (1.0 + gate_act * (1.0 - sig_gate))).astype(
        brain_float_sixteen
    )
    d_up = (d_hidden * silu_gate).astype(brain_float_sixteen)
    grad_gate_w = jnp.einsum("sqd,sqf->df", second_normed, d_gate, preferred_element_type=f32)
    grad_up_w = jnp.einsum("sqd,sqf->df", second_normed, d_up, preferred_element_type=f32)
    second_normed_gradient = input_sum(
        jnp.einsum("sqf,df->sqd", d_gate, gate_all, preferred_element_type=f32)
        + jnp.einsum("sqf,df->sqd", d_up, up_all, preferred_element_type=f32)
    )
    feedforward_scale_gradient, middle_gradient = norm_backward_pass(
        second_normed_gradient, second_unit_rows, second_inverse_root, feedforward_norm_scale
    )
    middle_gradient = middle_gradient + out_grad.astype(f32)
    grad_attn_rows = spread_grads(middle_gradient.astype(brain_float_sixteen))
    d_attn = jnp.einsum(
        "sqd,dh->sqh", grad_attn_rows, output_all, preferred_element_type=f32
    ).astype(brain_float_sixteen)
    grad_output_w = jnp.einsum("sqd,sqh->dh", grad_attn_rows, attn_out, preferred_element_type=f32)
    d_heads = jnp.moveaxis(d_attn.reshape(seq_count, query_rows, heads_here, HD), 2, 0)

    def backward_head(accumulated, operands):
        query_head, d_head, log_sum, group_id = operands
        masked, keys_group, values_group = scores_of(query_head, group_id)
        probs_f = jnp.exp(masked - log_sum[..., None])
        d_prob = jnp.einsum("sqd,skd->sqk", d_head, values_group, preferred_element_type=f32)
        row_delta = jnp.sum(probs_f * d_prob, -1, keepdims=True)
        d_score = (probs_f * (d_prob - row_delta)).astype(brain_float_sixteen)
        d_query = (
            jnp.einsum("sqk,skd->sqd", d_score, keys_group, preferred_element_type=f32) * inv_root
        )
        d_key = (
            jnp.einsum("sqk,sqd->skd", d_score, query_head, preferred_element_type=f32) * inv_root
        )
        d_value = jnp.einsum(
            "sqk,sqd->skd", probs_f.astype(brain_float_sixteen), d_head, preferred_element_type=f32
        )
        current = lax.dynamic_index_in_dim(accumulated, group_id, 2, keepdims=False)
        accumulated = lax.dynamic_update_index_in_dim(
            accumulated, current + jnp.concatenate([d_key, d_value], -1), group_id, 2
        )
        return (accumulated, d_query)

    zero_grads = jnp.zeros((seq_count, length, groups_here, 2 * HD), f32)
    d_keyval_seq, d_queries = lax.scan(
        backward_head, zero_grads, (query_heads, d_heads, log_sums, group_ids)
    )
    d_keyval = lax.psum_scatter(
        d_keyval_seq.reshape(seq_count, length, groups_here * 2 * HD),
        "ctx",
        scatter_dimension=1,
        tiled=True,
    ).reshape(seq_count, query_rows, groups_here, 2 * HD)
    d_keyval_raw = (
        jnp.concatenate(
            [unrotate(d_keyval[..., :HD], cosine_table, sine_table), d_keyval[..., HD:]], -1
        )
        .astype(brain_float_sixteen)
        .reshape(seq_count, query_rows, groups_here * 2 * HD)
    )
    d_query_raw = (
        unrotate(jnp.moveaxis(d_queries, 0, 2), cosine_table, sine_table)
        .astype(brain_float_sixteen)
        .reshape(seq_count, query_rows, heads_here * HD)
    )
    grad_query_w = jnp.einsum("sqd,sqh->dh", first_normed, d_query_raw, preferred_element_type=f32)
    grad_keyval_w = jnp.einsum(
        "sqd,sqh->dh", first_normed, d_keyval_raw, preferred_element_type=f32
    )
    first_normed_gradient = input_sum(
        jnp.einsum("sqh,dh->sqd", d_query_raw, query_all, preferred_element_type=f32)
        + jnp.einsum("sqh,dh->sqd", d_keyval_raw, keyval_all, preferred_element_type=f32)
    )
    attention_scale_gradient, residual_gradient = norm_backward_pass(
        first_normed_gradient, first_unit_rows, first_inverse_root, attention_norm_scale
    )
    input_grad = middle_gradient + residual_gradient
    gain_a_sum, grad_query, grad_keyval, grad_output = (
        lax.psum_scatter(
            attention_scale_gradient, ("shard", "ctx"), scatter_dimension=0, tiled=True
        ),
        lax.psum_scatter(grad_query_w, ("shard", "ctx"), scatter_dimension=0, tiled=True),
        lax.psum_scatter(grad_keyval_w, ("shard", "ctx"), scatter_dimension=0, tiled=True),
        lax.psum_scatter(grad_output_w, ("shard", "ctx"), scatter_dimension=0, tiled=True),
    )
    gain_m_sum, grad_gate, grad_up, grad_down = (
        lax.psum_scatter(
            feedforward_scale_gradient, ("shard", "ctx"), scatter_dimension=0, tiled=True
        ),
        lax.psum_scatter(grad_gate_w, ("shard", "ctx"), scatter_dimension=0, tiled=True),
        lax.psum_scatter(grad_up_w, ("shard", "ctx"), scatter_dimension=0, tiled=True),
        lax.psum_scatter(grad_down_w, ("shard", "ctx"), scatter_dimension=0, tiled=True),
    )
    grad_gain_attn, grad_gain_mlp = lax.psum((gain_a_sum, gain_m_sum), "tensor")
    return (
        layer_out,
        input_grad,
        grad_gain_attn,
        grad_query,
        grad_keyval,
        grad_output,
        grad_gain_mlp,
        grad_gate,
        grad_up,
        grad_down,
    )


def solution(mesh):
    return jax.shard_map(
        body,
        mesh=mesh,
        in_specs=(
            P("shard", ("ctx", "tensor"), None),
            P("shard", ("ctx", "tensor"), None),
            P("shard", None),
            P(("shard", "ctx")),
            P(("shard", "ctx"), "tensor"),
            P(("shard", "ctx"), "tensor"),
            P(("shard", "ctx"), "tensor"),
            P(("shard", "ctx")),
            P(("shard", "ctx"), "tensor"),
            P(("shard", "ctx"), "tensor"),
            P(("shard", "ctx"), "tensor"),
        ),
        out_specs=(
            P("shard", ("ctx", "tensor"), None),
            P("shard", ("ctx", "tensor"), None),
            P(("shard", "ctx")),
            P(("shard", "ctx"), "tensor"),
            P(("shard", "ctx"), "tensor"),
            P(("shard", "ctx"), "tensor"),
            P(("shard", "ctx")),
            P(("shard", "ctx"), "tensor"),
            P(("shard", "ctx"), "tensor"),
            P(("shard", "ctx"), "tensor"),
        ),
        check_vma=False,
    )
```

profile of v0, /device:TPU:0, one launch (start us, length us, event | category | flops | bytes accessed | tf_op | source)
XLA Modules:
  0.0 1319.3 jit_solution(5621312489691871391)
XLA Ops:
  7.9 14.8 %all-gather.1 = bf16[8,1,256]{2,1,0:T(2,128)(2,1)S(1)} all-gather(bf16[1,1,256]{2,1,0:T(2,128)(2,1)S(1)} %reshape.754), channel_id=1, replica_groups=mesh['shard'=2,'ctx'=4,'tensor'=4] {'shard','ctx'}, dimensions={0}, use_global_device_ids=true | all-gather | bytes 4608 | tf_op jit(solution)/shard_map/all_gather | solution.py:109
  29.0 26.2 %all_gather.50 = bf16[2048,128]{1,0:T(8,128)(2,1)S(1)} all-gather(bf16[256,128]{1,0:T(8,128)(2,1)} %param.20), channel_id=1, replica_groups=mesh['shard'=2,'ctx'=4,'tensor'=4] {'shard','ctx'}, dimensions={0}, use_global_device_ids=true | all-gather | bytes 589824 | tf_op jit(solution)/shard_map/all_gather | solution.py:111
  55.5 18.2 %all-gather.13.cloned.1.call-done = bf16[1,512,2048]{2,1,0:T(8,128)(2,1)} async-done(((bf16[1,128,2048]{2,1,0:T(8,128)(2,1)}), bf16[1,512,2048]{2,1,0:T(8,128)(2,1)}) %all-gather.13.cloned.1.call-update) | async-done | bytes 2097168 | tf_op jit(solution)/shard_map/all_gather | solution.py:61
  76.5 12.3 all-gather
  89.2 13.1 all-gather.15.cloned.1.call-done
  110.7 29.5 %while.28 = (s32[]{:T(128)}, bf16[8,1,512,64]{2,3,1,0:T(8,128)(2,1)S(1)}, f32[8,1,512]{2,1,0:T(1,128)S(1)}, bf16[8,1,512,64]{3,2,1,0:T(8,128)(2,1)}, bf16[1,2048...) while((s32[]{:T(128)}, ...), condition=%wide.region_5.6_spmd.clone, body=%wide.region_2.5_spmd.clone.sunk | while | flops 277904896 | bytes 13859421 | solution.py:164
  146.0 13.7 %all-gather.2 = bf16[8,1,256]{2,1,0:T(2,128)(2,1)S(1)} all-gather(bf16[1,1,256]{2,1,0:T(2,128)(2,1)S(1)} %reshape.756), channel_id=1, replica_groups=mesh['shard'=2,'ctx'=4,'tensor'=4] {'shard','ctx'}, dimensions={0}, use_global_device_ids=true | all-gather | bytes 4608 | tf_op jit(solution)/shard_map/all_gather | solution.py:115
  159.8 62.6 %reduce-scatter.12.cloned.1.call-done = f32[1,128,2048]{2,1,0:T(8,128)} async-done(((f32[1,512,2048]{2,1,0:T(8,128)}), f32[1,128,2048]{2,1,0:T(8,128)}) %reduce-scatter.12.cloned.1.call-update) | async-done | bytes 1048592 | tf_op jit(solution)/shard_map/reduce_scatter | solution.py:69
  227.7 40.3 %all-gather.23.cloned.1.call-done = bf16[2048,1408]{1,0:T(8,128)(2,1)} async-done(((bf16[256,1408]{1,0:T(8,128)(2,1)}), bf16[2048,1408]{1,0:T(8,128)(2,1)}) %all-gather.23.cloned.1.call-update) | async-done | bytes 5767184 | tf_op jit(solution)/shard_map/all_gather | solution.py:117
  268.1 48.0 %all-gather.19.cloned.1.call-done = bf16[1,512,2048]{2,1,0:T(8,128)(2,1)} async-done(((bf16[1,128,2048]{2,1,0:T(8,128)(2,1)}), bf16[1,512,2048]{2,1,0:T(8,128)(2,1)}) %all-gather.19.cloned.1.call-update) | async-done | bytes 2097168 | tf_op jit(solution)/shard_map/all_gather | solution.py:61
  324.4 35.8 %all-gather.21.cloned.1.call-done = bf16[2048,1408]{1,0:T(8,128)(2,1)} async-done(((bf16[256,1408]{1,0:T(8,128)(2,1)}), bf16[2048,1408]{1,0:T(8,128)(2,1)}) %all-gather.21.cloned.1.call-update) | async-done | bytes 5767184 | tf_op jit(solution)/shard_map/all_gather | solution.py:116
  368.4 39.4 %all-gather.27.cloned.1.call-done = bf16[1,512,2048]{2,1,0:T(8,128)(2,1)} async-done(((bf16[1,128,2048]{2,1,0:T(8,128)(2,1)}), bf16[1,512,2048]{2,1,0:T(8,128)(2,1)}) %all-gather.27.cloned.1.call-update) | async-done | bytes 2097168 | tf_op jit(solution)/shard_map/all_gather | solution.py:65
  407.8 44.1 %all-gather.25.cloned.1.call-done = bf16[2048,1408]{1,0:T(8,128)(2,1)} async-done(((bf16[256,1408]{1,0:T(8,128)(2,1)}), bf16[2048,1408]{1,0:T(8,128)(2,1)}) %all-gather.25.cloned.1.call-update) | async-done | bytes 5767184 | tf_op jit(solution)/shard_map/all_gather | solution.py:118
  451.9 10.4 multiply_convert_fusion.1
  473.6 76.9 %reduce-scatter.16.cloned.1.call-done = f32[1,128,2048]{2,1,0:T(8,128)} async-done(((f32[1,512,2048]{2,1,0:T(8,128)}), f32[1,128,2048]{2,1,0:T(8,128)}) %reduce-scatter.16.cloned.1.call-update) | async-done | bytes 1048592 | tf_op jit(solution)/shard_map/reduce_scatter | solution.py:73
  554.7 46.4 %all-gather.29.cloned.1.call-done = bf16[1,512,2048]{2,1,0:T(8,128)(2,1)} async-done(((bf16[1,128,2048]{2,1,0:T(8,128)(2,1)}), bf16[1,512,2048]{2,1,0:T(8,128)(2,1)}) %all-gather.29.cloned.1.call-update) | async-done | bytes 2097168 | tf_op jit(solution)/shard_map/all_gather | solution.py:65
  605.9 96.6 %while.29 = (s32[]{:T(128)}, f32[1,2048,1,128]{1,3,2,0:T(8,128)}, f32[8,1,512,64]{2,3,1,0:T(8,128)}, bf16[8,1,512,64]{3,2,1,0:T(8,128)(2,1)}, bf16[1,2048,1,128]...) while((s32[]{:T(128)}, f32[1,2048,1,128]{1,3,2,0:T(8,128)}, ...), condition=%wide.region_13.14_spmd.clone, body=%wide.region_11.13_spmd.clone.sunk | while | flops 682524160 | bytes 37902968 | solution.py:242
  702.7 9.5 convolution_bitcast_fusion.1
  717.5 11.7 reduce-scatter.18.cloned.1.call-done
  737.5 8.5 convolution_bitcast_fusion.2
  750.0 9.9 fusion.39
  760.0 10.4 fusion.37
  782.2 37.7 %reduce-scatter.32.cloned.1.call-done = f32[256,1408]{0,1:T(8,128)} async-done(((f32[2048,1408]{0,1:T(8,128)}), f32[256,1408]{0,1:T(8,128)}) %reduce-scatter.32.cloned.1.call-update) | async-done | bytes 1441808 | tf_op jit(solution)/shard_map/reduce_scatter | solution.py:289
  822.8 76.1 %reduce-scatter.20.cloned.1.call-done = f32[1,128,2048]{2,1,0:T(8,128)} async-done(((f32[1,512,2048]{2,1,0:T(8,128)}), f32[1,128,2048]{2,1,0:T(8,128)}) %reduce-scatter.20.cloned.1.call-update) | async-done | bytes 1048592 | tf_op jit(solution)/shard_map/reduce_scatter | solution.py:73
  900.5 26.9 %all-reduce.2 = (f32[2048]{0:T(1024)S(1)}, f32[2048]{0:T(1024)S(1)}) all-reduce(f32[2048]{0:T(1024)S(1)} %get-tuple-element.284, f32[2048]{0:T(1024)S(1)} %get-tuple-element.282), channel_id=8, replica_groups=mesh['shard'=2,'ctx'=4,'tensor'=4] {'shard','ctx'}, use_global_device_ids=true, to_apply=%region_18.19.clone | all-reduce | flops 4096 | bytes 32768
  927.6 12.4 all-reduce.3
  939.9 38.7 %reduce-scatter.14.cloned.1.call-done = f32[1,128,2048]{2,1,0:T(8,128)} async-done(((f32[1,512,2048]{2,1,0:T(8,128)}), f32[1,128,2048]{2,1,0:T(8,128)}) %reduce-scatter.14.cloned.1.call-update) | async-done | bytes 1048592 | tf_op jit(solution)/shard_map/reduce_scatter | solution.py:69
  981.8 37.3 %reduce-scatter.24.cloned.1.call-done = f32[256,128]{1,0:T(8,128)} async-done(((f32[2048,128]{1,0:T(8,128)}), f32[256,128]{1,0:T(8,128)}) %reduce-scatter.24.cloned.1.call-update) | async-done | bytes 131088 | tf_op jit(solution)/shard_map/reduce_scatter | solution.py:280
  1019.1 91.1 %reduce-scatter.28.cloned.1.call-done = f32[256,1408]{1,0:T(8,128)} async-done(((f32[2048,1408]{1,0:T(8,128)}), f32[256,1408]{1,0:T(8,128)}) %reduce-scatter.28.cloned.1.call-update) | async-done | bytes 1441808 | tf_op jit(solution)/shard_map/reduce_scatter | solution.py:287
  1110.3 91.1 %reduce-scatter.30.cloned.1.call-done = f32[256,1408]{1,0:T(8,128)} async-done(((f32[2048,1408]{1,0:T(8,128)}), f32[256,1408]{1,0:T(8,128)}) %reduce-scatter.30.cloned.1.call-update) | async-done | bytes 1441808 | tf_op jit(solution)/shard_map/reduce_scatter | solution.py:288
  1201.4 55.6 %reduce-scatter.26.cloned.1.call-done = f32[256,512]{1,0:T(8,128)} async-done(((f32[2048,512]{1,0:T(8,128)}), f32[256,512]{1,0:T(8,128)}) %reduce-scatter.26.cloned.1.call-update) | async-done | bytes 524304 | tf_op jit(solution)/shard_map/reduce_scatter | solution.py:281
  1257.0 55.1 %reduce-scatter.22.cloned.1.call-done = f32[256,512]{1,0:T(8,128)} async-done(((f32[2048,512]{1,0:T(8,128)}), f32[256,512]{1,0:T(8,128)}) %reduce-scatter.22.cloned.1.call-update) | async-done | bytes 524304 | tf_op jit(solution)/shard_map/reduce_scatter | solution.py:279
  (260 shorter events, 228.7 us)
Async XLA Ops:
  7.2 66.6 %all-gather.13.cloned.1.call-start = ((), (), s32[]{:S(2)}) async-start(), calls=%async_computation.11 | async-start | bytes 2621440 | tf_op jit(solution)/shard_map/all_gather | solution.py:61
  26.5 75.8 %all-gather.15.cloned.1.call-start = ((), (), s32[]{:S(2)}) async-start(), calls=%async_computation.12 | async-start | bytes 2359296 | tf_op jit(solution)/shard_map/all_gather | solution.py:110
  27.3 113.0 %all-gather.17.cloned.1.call-start = ((), (), s32[]{:S(2)}) async-start(), calls=%async_computation.13 | async-start | bytes 2359296 | tf_op jit(solution)/shard_map/all_gather | solution.py:112
  28.0 194.3 %reduce-scatter.12.cloned.1.call-start = ((), (), s32[]{:S(2)}) async-start(), calls=%async_computation.14 | async-start | bytes 5242880 | tf_op jit(solution)/shard_map/reduce_scatter | solution.py:69
  28.1 61.1 %copy-start.21 = (f32[32]{0:T(128)}, f32[32]{0:T(128)S(1)}, u32[]{:S(2)}) copy-start(f32[32]{0:T(128)S(1)} %multiply_power_fusion) | copy-start | bytes 388
  29.0 60.2 %copy-start.17 = (f32[1,512]{1,0:T(1,128)}, f32[1,512]{1,0:T(1,128)S(1)}, u32[]{:S(2)}) copy-start(f32[1,512]{1,0:T(1,128)S(1)} %fusion.96) | copy-start | bytes 6148
  76.5 29.7 %copy-start = (bf16[1,512,2048]{2,1,0:T(8,128)(2,1)S(1)}, bf16[1,512,2048]{2,1,0:T(8,128)(2,1)}, u32[]{:S(2)}) copy-start(bf16[1,512,2048]{2,1,0:T(8,128)(2,1)} %all-gather.13.cloned.1.call-done) | copy-start | bytes 6291460
  145.4 77.0 %copy-start.4 = (bf16[1,128,2048]{2,1,0:T(8,128)(2,1)S(1)}, bf16[1,128,2048]{2,1,0:T(8,128)(2,1)}, u32[]{:S(2)}) copy-start(bf16[1,128,2048]{2,1,0:T(8,128)(2,1)} %param.15) | copy-start | bytes 1572868
  145.4 122.7 %all-gather.23.cloned.1.call-start = ((), (), s32[]{:S(2)}) async-start(), calls=%async_computation.17 | async-start | bytes 6488064 | tf_op jit(solution)/shard_map/all_gather | solution.py:117
  146.0 170.1 %all-gather.19.cloned.1.call-start = ((), (), s32[]{:S(2)}) async-start(), calls=%async_computation.15 | async-start | bytes 2621440 | tf_op jit(solution)/shard_map/all_gather | solution.py:61
  223.8 328.3 %copy-start.2 = (f32[1,128,2048]{2,1,0:T(8,128)}, f32[1,128,2048]{2,1,0:T(8,128)S(1)}, u32[]{:S(2)}) copy-start(f32[1,128,2048]{2,1,0:T(8,128)S(1)} %get-tuple-element.323) | copy-start | bytes 3145732
  224.9 135.3 %all-gather.21.cloned.1.call-start = ((), (), s32[]{:S(2)}) async-start(), calls=%async_computation.16 | async-start | bytes 6488064 | tf_op jit(solution)/shard_map/all_gather | solution.py:116
  225.7 182.2 %all-gather.27.cloned.1.call-start = ((), (), s32[]{:S(2)}) async-start(), calls=%async_computation.20 | async-start | bytes 2621440 | tf_op jit(solution)/shard_map/all_gather | solution.py:65
  226.4 225.5 %all-gather.25.cloned.1.call-start = ((), (), s32[]{:S(2)}) async-start(), calls=%async_computation.18 | async-start | bytes 6488064 | tf_op jit(solution)/shard_map/all_gather | solution.py:118
  227.1 323.3 %reduce-scatter.16.cloned.1.call-start = ((), (), s32[]{:S(2)}) async-start(), calls=%async_computation.21 | async-start | bytes 5242880 | tf_op jit(solution)/shard_map/reduce_scatter | solution.py:73
  473.5 78.5 %copy-start.8 = (bf16[1,128,2048]{2,1,0:T(8,128)(2,1)S(1)}, bf16[1,128,2048]{2,1,0:T(8,128)(2,1)}, u32[]{:S(2)}) copy-start(bf16[1,128,2048]{2,1,0:T(8,128)(2,1)} %param.16) | copy-start | bytes 1572868
  473.5 127.5 %all-gather.29.cloned.1.call-start = ((), (), s32[]{:S(2)}) async-start(), calls=%async_computation.22 | async-start | bytes 2621440 | tf_op jit(solution)/shard_map/all_gather | solution.py:65
  554.4 174.8 %reduce-scatter.18.cloned.1.call-start = ((), (), s32[]{:S(2)}) async-start(), calls=%async_computation.23 | async-start | bytes 1310720 | tf_op jit(solution)/shard_map/reduce_scatter | solution.py:245
  702.6 117.3 %reduce-scatter.32.cloned.1.call-start = ((), (), s32[]{:S(2)}) async-start(), calls=%async_computation.30 | async-start | bytes 12976128 | tf_op jit(solution)/shard_map/reduce_scatter | solution.py:289
  712.2 186.7 %reduce-scatter.20.cloned.1.call-start = ((), (), s32[]{:S(2)}) async-start(), calls=%async_computation.24 | async-start | bytes 5242880 | tf_op jit(solution)/shard_map/reduce_scatter | solution.py:73
  736.2 242.5 %reduce-scatter.14.cloned.1.call-start = ((), (), s32[]{:S(2)}) async-start(), calls=%async_computation.19 | async-start | bytes 5242880 | tf_op jit(solution)/shard_map/reduce_scatter | solution.py:69
  746.1 273.0 %reduce-scatter.24.cloned.1.call-start = ((), (), s32[]{:S(2)}) async-start(), calls=%async_computation.26 | async-start | bytes 1179648 | tf_op jit(solution)/shard_map/reduce_scatter | solution.py:280
  750.0 360.3 %reduce-scatter.28.cloned.1.call-start = ((), (), s32[]{:S(2)}) async-start(), calls=%async_computation.28 | async-start | bytes 12976128 | tf_op jit(solution)/shard_map/reduce_scatter | solution.py:287
  759.9 441.4 %reduce-scatter.30.cloned.1.call-start = ((), (), s32[]{:S(2)}) async-start(), calls=%async_computation.29 | async-start | bytes 12976128 | tf_op jit(solution)/shard_map/reduce_scatter | solution.py:288
  770.4 486.6 %reduce-scatter.26.cloned.1.call-start = ((), (), s32[]{:S(2)}) async-start(), calls=%async_computation.27 | async-start | bytes 4718592 | tf_op jit(solution)/shard_map/reduce_scatter | solution.py:281
  776.6 535.5 %reduce-scatter.22.cloned.1.call-start = ((), (), s32[]{:S(2)}) async-start(), calls=%async_computation.25 | async-start | bytes 4718592 | tf_op jit(solution)/shard_map/reduce_scatter | solution.py:279
  780.3 118.6 %copy-start.5 = (bf16[1,128,2048]{2,1,0:T(8,128)(2,1)S(1)}, bf16[1,128,2048]{2,1,0:T(8,128)(2,1)}, u32[]{:S(2)}) copy-start(bf16[1,128,2048]{2,1,0:T(8,128)(2,1)} %param.15) | copy-start | bytes 1572868
  780.3 118.6 %copy-start.16 = (f32[8,1,256]{2,1,0:T(1,128)S(1)}, f32[8,1,256]{2,1,0:T(1,128)}, u32[]{:S(2)}) copy-start(f32[8,1,256]{2,1,0:T(1,128)} %copy-done.15) | copy-start | bytes 24580
  780.3 118.6 %copy-start.20 = (f32[128]{0:T(128)S(1)}, f32[128]{0:T(128)}, u32[]{:S(2)}) copy-start(f32[128]{0:T(128)} %copy-done.19) | copy-start | bytes 1540
  780.4 198.3 %copy-start.3 = (f32[1,128,2048]{2,1,0:T(8,128)S(1)}, f32[1,128,2048]{2,1,0:T(8,128)}, u32[]{:S(2)}) copy-start(f32[1,128,2048]{2,1,0:T(8,128)} %copy-done.2) | copy-start | bytes 3145732
  780.4 198.3 %copy-start.6 = (f32[1,128,2048]{2,1,0:T(8,128)S(1)}, f32[1,128,2048]{2,1,0:T(8,128)}, u32[]{:S(2)}) copy-start(f32[1,128,2048]{2,1,0:T(8,128)} %reduce-scatter.16.cloned.1.call-done) | copy-start | bytes 3145732
  780.4 198.3 %copy-start.9 = (bf16[1,128,2048]{2,1,0:T(8,128)(2,1)S(1)}, bf16[1,128,2048]{2,1,0:T(8,128)(2,1)}, u32[]{:S(2)}) copy-start(bf16[1,128,2048]{2,1,0:T(8,128)(2,1)} %param.16) | copy-start | bytes 1572868
  (17 other events, 102.2 us)
Sparse Core Ops, SparseCore 0:
  26.6 47.0 all-gather.12
  75.6 26.6 all-gather.14
  104.2 27.8 all-gather.16
  145.5 76.7 reduce-scatter.11
  224.2 43.8 all-gather.22
  270.1 45.9 all-gather.18
  318.1 42.0 all-gather.20
  361.9 45.9 all-gather.26
  409.9 42.0 all-gather.24
  473.7 76.7 reduce-scatter.15
  554.6 46.4 all-gather.28
  702.7 26.4 reduce-scatter.17
  733.1 86.7 reduce-scatter.31
  822.2 76.7 reduce-scatter.19
  901.1 77.5 reduce-scatter.13
  982.6 36.4 reduce-scatter.23
  1023.4 86.7 reduce-scatter.27
  1114.6 86.7 reduce-scatter.29
  1205.7 51.2 reduce-scatter.25
  1260.8 51.3 reduce-scatter.21
where the time goes:
time: 1330 us; the launch traced here: 1320 us
  waiting for transfers between devices  924 us (69%)
  matrix products  206 us (15%)
  blocking collectives  106 us (8%)
  other arithmetic  47.6 us (4%)
  local copies, waits for them, and re-layouts  18.1 us (1%)
  between operations  15.7 us (1%)
    reduce_scatter x2, waiting for transfers between devices, input_sum(): lax.psum_scatter(partial_sum, 'tensor', scatter_dimension=1, tiled=True)  153 us
    reduce_scatter x2, waiting for transfers between devices, branch_sum(): lax.psum_scatter(partial_sum, 'tensor', scatter_dimension=1, tiled=True)  101 us
    reduce_scatter x1, waiting for transfers between devices, body(): lax.psum_scatter(grad_gate_w, ('shard', 'ctx'), scatter_dimension=0, tile...  91.1 us
    reduce_scatter x1, waiting for transfers between devices, body(): lax.psum_scatter(grad_up_w, ('shard', 'ctx'), scatter_dimension=0, tiled=...  91.1 us
    all_gather x2, waiting for transfers between devices, spread_grads(): return lax.all_gather(values_in, 'tensor', axis=1, tiled=True)  85.8 us
    all_gather x2, waiting for transfers between devices, broadcast_rows(): return lax.all_gather(values_in, 'tensor', axis=1, tiled=True)  66.3 us
    reduce_scatter x1, waiting for transfers between devices, body(): lax.psum_scatter(grad_output_w, ('shard', 'ctx'), scatter_dimension=0, ti...  55.6 us
    reduce_scatter x1, waiting for transfers between devices, body(): lax.psum_scatter(grad_query_w, ('shard', 'ctx'), scatter_dimension=0, til...  55.1 us
  transfers between devices with their start and end apart: 20, of which 19 were waited for; matrix products, arithmetic and copies ran while one was open for 10% of the time, Pallas kernels for 0%

commit v1 on v0

--- a/solution.py
+++ b/solution.py
@@ -8,6 +8,27 @@
 BLOCKS = 8
 epsilon = 1e-05
 blocked = -1e30
+
+
+def collect(array, axis, dim):
+    peers, here, rows = (lax.axis_size(axis), lax.axis_index(axis), array.shape[dim])
+    upward = [(i, (i + 1) % peers) for i in range(peers)]
+    left = [(i, (i - 1) % peers) for i in range(peers)]
+    out = jnp.zeros((*array.shape[:dim], peers * rows, *array.shape[dim + 1 :]), array.dtype)
+    out = lax.dynamic_update_slice_in_dim(out, array, here * rows, axis=dim)
+    from_left = from_right = array
+    half = peers // 2
+    for step in range(1, half + 1):
+        from_left = lax.ppermute(from_left, axis, upward)
+        out = lax.dynamic_update_slice_in_dim(
+            out, from_left, (here - step) % peers * rows, axis=dim
+        )
+        if step < peers - half:
+            from_right = lax.ppermute(from_right, axis, left)
+            out = lax.dynamic_update_slice_in_dim(
+                out, from_right, (here + step) % peers * rows, axis=dim
+            )
+    return out
 
 
 def apply_norm(values_in):
@@ -62,7 +83,7 @@
 
 
 def spread_grads(values_in):
-    return lax.all_gather(values_in, "tensor", axis=1, tiled=True)
+    return collect(values_in, "tensor", 1)
 
 
 def branch_sum(partial_sum):

time: 1330 us -> 1280 us (0.962)
  waiting for transfers between devices: 924 us -> 853 us
  starting transfers between devices: 1.97 us -> 27.1 us
    all_gather x2 -> x0, waiting for transfers between devices: 85.8 us -> none  [spread_grads(): return lax.all_gather(values_in, 'tensor', axis=1, tiled=True)]
    reduce_scatter x1, waiting for transfers between devices: 37.7 us -> 91.1 us  [body(): lax.psum_scatter(grad_down_w, ('shard', 'ctx'), scatter_dimension=0, tile...]
    reduce_scatter x2, waiting for transfers between devices: 153 us -> 105 us  [input_sum(): lax.psum_scatter(partial_sum, 'tensor', scatter_dimension=1, tiled=True)]
    ppermute x0 -> x6, waiting for transfers between devices: none -> 44.1 us  [the longest x4 43.2 us: collect(): from_left = lax.ppermute(from_left, axis, upward)]
    all_gather x1, waiting for transfers between devices: 40.3 us -> 2.85 us  [body(): lax.all_gather(w_up, ('shard', 'ctx'), axis=0, tiled=True)]
    ppermute x0 -> x6, starting transfers between devices: none -> 26.2 us  [the longest x4 21.5 us: collect(): from_left = lax.ppermute(from_left, axis, upward)]
  transfers between devices with their start and end apart: 20 -> 24, of which waited for: 19 -> 23; matrix products, arithmetic and copies ran while one was open for 10% -> 9% of each run, Pallas kernels for 0% -> 0%
where the time goes in v1:
time: 1280 us; the launch traced here: 1270 us
  waiting for transfers between devices  853 us (67%)
  matrix products  197 us (15%)
  blocking collectives  106 us (8%)
  other arithmetic  44.8 us (4%)
  starting transfers between devices  27.1 us (2%)
  local copies, waits for them, and re-layouts  25.2 us (2%)
  between operations  15.6 us (1%)
    reduce_scatter x2, waiting for transfers between devices, input_sum(): lax.psum_scatter(partial_sum, 'tensor', scatter_dimension=1, tiled=True)  105 us
    reduce_scatter x2, waiting for transfers between devices, branch_sum(): lax.psum_scatter(partial_sum, 'tensor', scatter_dimension=1, tiled=True)  101 us
    reduce_scatter x1, waiting for transfers between devices, body(): lax.psum_scatter(grad_gate_w, ('shard', 'ctx'), scatter_dimension=0, tile...  91.1 us
    reduce_scatter x1, waiting for transfers between devices, body(): lax.psum_scatter(grad_down_w, ('shard', 'ctx'), scatter_dimension=0, tile...  91.1 us
    reduce_scatter x1, waiting for transfers between devices, body(): lax.psum_scatter(grad_up_w, ('shard', 'ctx'), scatter_dimension=0, tiled=...  91.1 us
    all_gather x2, waiting for transfers between devices, broadcast_rows(): return lax.all_gather(values_in, 'tensor', axis=1, tiled=True)  66.8 us
    reduce_scatter x1, waiting for transfers between devices, body(): lax.psum_scatter(grad_output_w, ('shard', 'ctx'), scatter_dimension=0, ti...  55.5 us
    reduce_scatter x1, waiting for transfers between devices, body(): lax.psum_scatter(grad_query_w, ('shard', 'ctx'), scatter_dimension=0, til...  55.1 us
  transfers between devices with their start and end apart: 24, of which 23 were waited for; matrix products, arithmetic and copies ran while one was open for 9% of the time, Pallas kernels for 0%

profile of v1, /device:TPU:0, one launch (start us, length us, event | category | flops | bytes accessed | tf_op | source)
XLA Modules:
  0.0 1269.6 jit_solution(16839509110044913879)
XLA Ops:
  7.9 14.8 %all-gather.1 = bf16[8,1,256]{2,1,0:T(2,128)(2,1)S(1)} all-gather(bf16[1,1,256]{2,1,0:T(2,128)(2,1)S(1)} %reshape.788), channel_id=1, replica_groups=mesh['shard'=2,'ctx'=4,'tensor'=4] {'shard','ctx'}, dimensions={0}, use_global_device_ids=true | all-gather | bytes 4608 | tf_op jit(solution)/shard_map/all_gather | solution.py:130
  27.9 26.3 %all_gather.44 = bf16[2048,128]{1,0:T(8,128)(2,1)S(1)} all-gather(bf16[256,128]{1,0:T(8,128)(2,1)S(1)} %copy-done.18), channel_id=1, replica_groups=mesh['shard'=2,'ctx'=4,'tensor'=4] {'shard','ctx'}, dimensions={0}, use_global_device_ids=true | all-gather | bytes 589824 | tf_op jit(solution)/shard_map/all_gather | solution.py:132
  54.5 18.8 %all-gather.11.cloned.1.call-done = bf16[1,512,2048]{2,1,0:T(8,128)(2,1)} async-done(((bf16[1,128,2048]{2,1,0:T(8,128)(2,1)}), bf16[1,512,2048]{2,1,0:T(8,128)(2,1)}) %all-gather.11.cloned.1.call-update) | async-done | bytes 2097168 | tf_op jit(solution)/shard_map/all_gather | solution.py:82
  76.1 12.3 all-gather
  88.6 13.2 %all-gather.13.cloned.1.call-done = bf16[2048,512]{1,0:T(8,128)(2,1)} async-done(((bf16[256,512]{1,0:T(8,128)(2,1)}), bf16[2048,512]{1,0:T(8,128)(2,1)}) %all-gather.13.cloned.1.call-update) | async-done | bytes 2097168 | tf_op jit(solution)/shard_map/all_gather | solution.py:131
  110.3 29.6 %while.28 = (s32[]{:T(128)}, bf16[8,1,512,64]{2,3,1,0:T(8,128)(2,1)S(1)}, f32[8,1,512]{2,1,0:T(1,128)S(1)}, bf16[8,1,512,64]{3,2,1,0:T(8,128)(2,1)}, bf16[1,2048...) while((s32[]{:T(128)}, ...), condition=%wide.region_5.6_spmd.clone, body=%wide.region_2.5_spmd.clone.sunk | while | flops 277904896 | bytes 13859421 | solution.py:185
  145.7 13.7 %all-gather.2 = bf16[8,1,256]{2,1,0:T(2,128)(2,1)S(1)} all-gather(bf16[1,1,256]{2,1,0:T(2,128)(2,1)S(1)} %reshape.790), channel_id=1, replica_groups=mesh['shard'=2,'ctx'=4,'tensor'=4] {'shard','ctx'}, dimensions={0}, use_global_device_ids=true | all-gather | bytes 4608 | tf_op jit(solution)/shard_map/all_gather | solution.py:136
  159.4 62.6 %reduce-scatter.12.cloned.1.call-done = f32[1,128,2048]{2,1,0:T(8,128)} async-done(((f32[1,512,2048]{2,1,0:T(8,128)}), f32[1,128,2048]{2,1,0:T(8,128)}) %reduce-scatter.12.cloned.1.call-update) | async-done | bytes 1048592 | tf_op jit(solution)/shard_map/reduce_scatter | solution.py:90
  232.2 10.4 collective-permute-done
  242.6 9.4 collective-permute-start.2
  254.0 10.0 collective-permute-done.2
  267.6 48.0 %all-gather.17.cloned.1.call-done = bf16[1,512,2048]{2,1,0:T(8,128)(2,1)} async-done(((bf16[1,128,2048]{2,1,0:T(8,128)(2,1)}), bf16[1,512,2048]{2,1,0:T(8,128)(2,1)}) %all-gather.17.cloned.1.call-update) | async-done | bytes 2097168 | tf_op jit(solution)/shard_map/all_gather | solution.py:82
  315.7 8.3 fusion.34
  324.0 35.8 %all-gather.19.cloned.1.call-done = bf16[2048,1408]{1,0:T(8,128)(2,1)} async-done(((bf16[256,1408]{1,0:T(8,128)(2,1)}), bf16[2048,1408]{1,0:T(8,128)(2,1)}) %all-gather.19.cloned.1.call-update) | async-done | bytes 5767184 | tf_op jit(solution)/shard_map/all_gather | solution.py:137
  368.0 37.2 %all-gather.23.cloned.1.call-done = bf16[2048,1408]{1,0:T(8,128)(2,1)} async-done(((bf16[256,1408]{1,0:T(8,128)(2,1)}), bf16[2048,1408]{1,0:T(8,128)(2,1)}) %all-gather.23.cloned.1.call-update) | async-done | bytes 5767184 | tf_op jit(solution)/shard_map/all_gather | solution.py:139
  405.2 10.4 multiply_convert_fusion.1
  426.9 76.9 %reduce-scatter.16.cloned.1.call-done = f32[1,128,2048]{2,1,0:T(8,128)} async-done(((f32[1,512,2048]{2,1,0:T(8,128)}), f32[1,128,2048]{2,1,0:T(8,128)}) %reduce-scatter.16.cloned.1.call-update) | async-done | bytes 1048592 | tf_op jit(solution)/shard_map/reduce_scatter | solution.py:94
  511.2 12.8 %collective-permute-done.3 = bf16[1,128,2048]{2,1,0:T(8,128)(2,1)S(1)} collective-permute-done((bf16[1,128,2048]{2,1,0:T(8,128)(2,1)S(1)}, bf16[1,128,2048]{2,1,0:T(8,128)(2,1)S(1)}, u32[]{:S(2)}, u32[]{:S(2)}) %collective-permute-start.3) | collective-permute-done | bytes 524320 | tf_op jit(solution)/shard_map/ppermute | solution.py:22
  524.1 9.1 collective-permute-start.5
  535.5 10.0 collective-permute-done.5
  550.5 96.6 %while.29 = (s32[]{:T(128)}, f32[1,2048,1,128]{1,3,2,0:T(8,128)}, f32[8,1,512,64]{2,3,1,0:T(8,128)}, bf16[8,1,512,64]{3,2,1,0:T(8,128)(2,1)}, bf16[1,2048,1,128]...) while((s32[]{:T(128)}, f32[1,2048,1,128]{1,3,2,0:T(8,128)}, ...), condition=%wide.region_13.14_spmd.clone, body=%wide.region_11.13_spmd.clone.sunk | while | flops 682524160 | bytes 37902968 | solution.py:263
  652.3 21.9 %reduce-scatter.18.cloned.1.call-done = f32[1,512,128]{1,2,0:T(8,128)} async-done(((f32[1,2048,128]{1,2,0:T(8,128)}), f32[1,512,128]{1,2,0:T(8,128)}) %reduce-scatter.18.cloned.1.call-update) | async-done | bytes 262160 | tf_op jit(solution)/shard_map/reduce_scatter | solution.py:266
  730.1 28.1 %reduce-scatter.20.cloned.1.call-done = f32[1,128,2048]{2,1,0:T(8,128)} async-done(((f32[1,512,2048]{2,1,0:T(8,128)}), f32[1,128,2048]{2,1,0:T(8,128)}) %reduce-scatter.20.cloned.1.call-update) | async-done | bytes 1048592 | tf_op jit(solution)/shard_map/reduce_scatter | solution.py:94
  759.8 26.9 %all-reduce.2 = (f32[2048]{0:T(1024)S(1)}, f32[2048]{0:T(1024)S(1)}) all-reduce(f32[2048]{0:T(1024)S(1)} %get-tuple-element.244, f32[2048]{0:T(1024)S(1)} %get-tuple-element.242), channel_id=8, replica_groups=mesh['shard'=2,'ctx'=4,'tensor'=4] {'shard','ctx'}, use_global_device_ids=true, to_apply=%region_18.19.clone | all-reduce | flops 4096 | bytes 32768
  786.8 12.4 all-reduce.3
  799.1 38.7 %reduce-scatter.14.cloned.1.call-done = f32[1,128,2048]{2,1,0:T(8,128)} async-done(((f32[1,512,2048]{2,1,0:T(8,128)}), f32[1,128,2048]{2,1,0:T(8,128)}) %reduce-scatter.14.cloned.1.call-update) | async-done | bytes 1048592 | tf_op jit(solution)/shard_map/reduce_scatter | solution.py:90
  841.0 37.5 %reduce-scatter.24.cloned.1.call-done = f32[256,128]{1,0:T(8,128)} async-done(((f32[2048,128]{1,0:T(8,128)}), f32[256,128]{1,0:T(8,128)}) %reduce-scatter.24.cloned.1.call-update) | async-done | bytes 131088 | tf_op jit(solution)/shard_map/reduce_scatter | solution.py:301
  878.5 55.5 %reduce-scatter.26.cloned.1.call-done = f32[256,512]{1,0:T(8,128)} async-done(((f32[2048,512]{1,0:T(8,128)}), f32[256,512]{1,0:T(8,128)}) %reduce-scatter.26.cloned.1.call-update) | async-done | bytes 524304 | tf_op jit(solution)/shard_map/reduce_scatter | solution.py:302
  934.0 55.1 %reduce-scatter.22.cloned.1.call-done = f32[256,512]{1,0:T(8,128)} async-done(((f32[2048,512]{1,0:T(8,128)}), f32[256,512]{1,0:T(8,128)}) %reduce-scatter.22.cloned.1.call-update) | async-done | bytes 524304 | tf_op jit(solution)/shard_map/reduce_scatter | solution.py:300
  989.1 91.1 %reduce-scatter.28.cloned.1.call-done = f32[256,1408]{1,0:T(8,128)} async-done(((f32[2048,1408]{1,0:T(8,128)}), f32[256,1408]{1,0:T(8,128)}) %reduce-scatter.28.cloned.1.call-update) | async-done | bytes 1441808 | tf_op jit(solution)/shard_map/reduce_scatter | solution.py:308
  1080.3 91.1 %reduce-scatter.30.cloned.1.call-done = f32[256,1408]{1,0:T(8,128)} async-done(((f32[2048,1408]{1,0:T(8,128)}), f32[256,1408]{1,0:T(8,128)}) %reduce-scatter.30.cloned.1.call-update) | async-done | bytes 1441808 | tf_op jit(solution)/shard_map/reduce_scatter | solution.py:309
  1171.4 91.1 %reduce-scatter.32.cloned.1.call-done = f32[256,1408]{1,0:T(8,128)} async-done(((f32[2048,1408]{1,0:T(8,128)}), f32[256,1408]{1,0:T(8,128)}) %reduce-scatter.32.cloned.1.call-update) | async-done | bytes 1441808 | tf_op jit(solution)/shard_map/reduce_scatter | solution.py:310
  (286 shorter events, 264.2 us)
Async XLA Ops:
  7.2 66.1 %all-gather.11.cloned.1.call-start = ((), (), s32[]{:S(2)}) async-start(), calls=%async_computation.11 | async-start | bytes 2621440 | tf_op jit(solution)/shard_map/all_gather | solution.py:82
  26.0 75.7 %all-gather.13.cloned.1.call-start = ((), (), s32[]{:S(2)}) async-start(), calls=%async_computation.12 | async-start | bytes 2359296 | tf_op jit(solution)/shard_map/all_gather | solution.py:131
  26.8 113.1 %all-gather.15.cloned.1.call-start = ((), (), s32[]{:S(2)}) async-start(), calls=%async_computation.13 | async-start | bytes 2359296 | tf_op jit(solution)/shard_map/all_gather | solution.py:133
  27.5 194.4 %reduce-scatter.12.cloned.1.call-start = ((), (), s32[]{:S(2)}) async-start(), calls=%async_computation.14 | async-start | bytes 5242880 | tf_op jit(solution)/shard_map/reduce_scatter | solution.py:90
  27.6 48.4 %copy-start.23 = (f32[32]{0:T(128)}, f32[32]{0:T(128)S(1)}, u32[]{:S(2)}) copy-start(f32[32]{0:T(128)S(1)} %multiply_power_fusion) | copy-start | bytes 388
  27.9 48.2 %copy-start.19 = (f32[1,512]{1,0:T(1,128)}, f32[1,512]{1,0:T(1,128)S(1)}, u32[]{:S(2)}) copy-start(f32[1,512]{1,0:T(1,128)S(1)} %fusion.86) | copy-start | bytes 6148
  145.0 77.0 %copy-start.4 = (bf16[1,128,2048]{2,1,0:T(8,128)(2,1)S(1)}, bf16[1,128,2048]{2,1,0:T(8,128)(2,1)}, u32[]{:S(2)}) copy-start(bf16[1,128,2048]{2,1,0:T(8,128)(2,1)} %param.15) | copy-start | bytes 1572868
  145.0 122.6 %all-gather.21.cloned.1.call-start = ((), (), s32[]{:S(2)}) async-start(), calls=%async_computation.17 | async-start | bytes 6488064 | tf_op jit(solution)/shard_map/all_gather | solution.py:138
  145.6 170.1 %all-gather.17.cloned.1.call-start = ((), (), s32[]{:S(2)}) async-start(), calls=%async_computation.15 | async-start | bytes 2621440 | tf_op jit(solution)/shard_map/all_gather | solution.py:82
  223.4 282.3 %copy-start.2 = (f32[1,128,2048]{2,1,0:T(8,128)}, f32[1,128,2048]{2,1,0:T(8,128)S(1)}, u32[]{:S(2)}) copy-start(f32[1,128,2048]{2,1,0:T(8,128)S(1)} %get-tuple-element.285) | copy-start | bytes 3145732
  224.4 135.4 %all-gather.19.cloned.1.call-start = ((), (), s32[]{:S(2)}) async-start(), calls=%async_computation.16 | async-start | bytes 6488064 | tf_op jit(solution)/shard_map/all_gather | solution.py:137
  225.1 180.1 %all-gather.23.cloned.1.call-start = ((), (), s32[]{:S(2)}) async-start(), calls=%async_computation.18 | async-start | bytes 6488064 | tf_op jit(solution)/shard_map/all_gather | solution.py:139
  225.9 277.9 %reduce-scatter.16.cloned.1.call-start = ((), (), s32[]{:S(2)}) async-start(), calls=%async_computation.20 | async-start | bytes 5242880 | tf_op jit(solution)/shard_map/reduce_scatter | solution.py:94
  225.9 16.7 %collective-permute-start = (bf16[1,128,2048]{2,1,0:T(8,128)(2,1)S(1)}, bf16[1,128,2048]{2,1,0:T(8,128)(2,1)S(1)}, u32[]{:S(2)}, u32[]{:S(2)}) collective-permute-start(bf16[1,128,2048]{2,1,0:T(8,128)(2,1)S(1)} %copy-done.12), channel_id=1, source_target_pairs={{0,1},{1,2},{2,3},{3,0},{4,5},{5,6},{6,7},{7,4},{8,9},{9,10},{10,1... | collective-permute-start | bytes 1572872 | tf_op jit(solution)/shard_map/ppermute | solution.py:22
  227.5 25.7 %collective-permute-start.1 = (bf16[1,128,2048]{2,1,0:T(8,128)(2,1)S(1)}, bf16[1,128,2048]{2,1,0:T(8,128)(2,1)S(1)}, u32[]{:S(2)}, u32[]{:S(2)}) collective-permute-start(bf16[1,128,2048]{2,1,0:T(8,128)(2,1)S(1)} %copy-done.12), channel_id=1, source_target_pairs={{0,3},{1,0},{2,1},{3,2},{4,7},{5,4},{6,5},{7,6},{8,11},{9,8},{10,9... | collective-permute-start | bytes 1572872 | tf_op jit(solution)/shard_map/ppermute | solution.py:27
  242.6 21.4 %collective-permute-start.2 = (bf16[1,128,2048]{2,1,0:T(8,128)(2,1)S(1)}, bf16[1,128,2048]{2,1,0:T(8,128)(2,1)S(1)}, u32[]{:S(2)}, u32[]{:S(2)}) collective-permute-start(bf16[1,128,2048]{2,1,0:T(8,128)(2,1)S(1)} %collective-permute-done), channel_id=1, source_target_pairs={{0,1},{1,2},{2,3},{3,0},{4,5},{5,6},{6,7},{7,4},{8,9},{9,10},{10,1... | collective-permute-start | bytes 1572872 | tf_op jit(solution)/shard_map/ppermute | solution.py:22
  426.8 247.4 %reduce-scatter.18.cloned.1.call-start = ((), (), s32[]{:S(2)}) async-start(), calls=%async_computation.21 | async-start | bytes 1310720 | tf_op jit(solution)/shard_map/reduce_scatter | solution.py:266
  507.4 16.7 %collective-permute-start.3 = (bf16[1,128,2048]{2,1,0:T(8,128)(2,1)S(1)}, bf16[1,128,2048]{2,1,0:T(8,128)(2,1)S(1)}, u32[]{:S(2)}, u32[]{:S(2)}) collective-permute-start(bf16[1,128,2048]{2,1,0:T(8,128)(2,1)S(1)} %get-tuple-element.283), channel_id=1, source_target_pairs={{0,1},{1,2},{2,3},{3,0},{4,5},{5,6},{6,7},{7,4},{8,9},{9,10},{10,1... | collective-permute-start | bytes 1572872 | tf_op jit(solution)/shard_map/ppermute | solution.py:22
  508.9 25.7 %collective-permute-start.4 = (bf16[1,128,2048]{2,1,0:T(8,128)(2,1)S(1)}, bf16[1,128,2048]{2,1,0:T(8,128)(2,1)S(1)}, u32[]{:S(2)}, u32[]{:S(2)}) collective-permute-start(bf16[1,128,2048]{2,1,0:T(8,128)(2,1)S(1)} %get-tuple-element.283), channel_id=1, source_target_pairs={{0,3},{1,0},{2,1},{3,2},{4,7},{5,4},{6,5},{7,6},{8,11},{9,8},{10,9... | collective-permute-start | bytes 1572872 | tf_op jit(solution)/shard_map/ppermute | solution.py:27
  511.2 35.0 %copy-start.28 = (bf16[2048,512]{1,0:T(8,128)(2,1)S(1)}, bf16[2048,512]{1,0:T(8,128)(2,1)}, u32[]{:S(2)}) copy-start(bf16[2048,512]{1,0:T(8,128)(2,1)} %all-gather.15.cloned.1.call-done) | copy-start | bytes 6291460
  524.1 21.4 %collective-permute-start.5 = (bf16[1,128,2048]{2,1,0:T(8,128)(2,1)S(1)}, bf16[1,128,2048]{2,1,0:T(8,128)(2,1)S(1)}, u32[]{:S(2)}, u32[]{:S(2)}) collective-permute-start(bf16[1,128,2048]{2,1,0:T(8,128)(2,1)S(1)} %collective-permute-done.3), channel_id=1, source_target_pairs={{0,1},{1,2},{2,3},{3,0},{4,5},{5,6},{6,7},{7,4},{8,9},{9,10},{10,1... | collective-permute-start | bytes 1572872 | tf_op jit(solution)/shard_map/ppermute | solution.py:22
  647.1 111.0 %reduce-scatter.20.cloned.1.call-start = ((), (), s32[]{:S(2)}) async-start(), calls=%async_computation.22 | async-start | bytes 5242880 | tf_op jit(solution)/shard_map/reduce_scatter | solution.py:94
  681.2 156.6 %reduce-scatter.14.cloned.1.call-start = ((), (), s32[]{:S(2)}) async-start(), calls=%async_computation.19 | async-start | bytes 5242880 | tf_op jit(solution)/shard_map/reduce_scatter | solution.py:90
  690.2 188.3 %reduce-scatter.24.cloned.1.call-start = ((), (), s32[]{:S(2)}) async-start(), calls=%async_computation.24 | async-start | bytes 1179648 | tf_op jit(solution)/shard_map/reduce_scatter | solution.py:301
  693.5 240.5 %reduce-scatter.26.cloned.1.call-start = ((), (), s32[]{:S(2)}) async-start(), calls=%async_computation.25 | async-start | bytes 4718592 | tf_op jit(solution)/shard_map/reduce_scatter | solution.py:302
  698.4 290.7 %reduce-scatter.22.cloned.1.call-start = ((), (), s32[]{:S(2)}) async-start(), calls=%async_computation.23 | async-start | bytes 4718592 | tf_op jit(solution)/shard_map/reduce_scatter | solution.py:300
  702.1 378.2 %reduce-scatter.28.cloned.1.call-start = ((), (), s32[]{:S(2)}) async-start(), calls=%async_computation.26 | async-start | bytes 12976128 | tf_op jit(solution)/shard_map/reduce_scatter | solution.py:308
  711.2 460.1 %reduce-scatter.30.cloned.1.call-start = ((), (), s32[]{:S(2)}) async-start(), calls=%async_computation.27 | async-start | bytes 12976128 | tf_op jit(solution)/shard_map/reduce_scatter | solution.py:309
  718.9 543.6 %reduce-scatter.32.cloned.1.call-start = ((), (), s32[]{:S(2)}) async-start(), calls=%async_computation.28 | async-start | bytes 12976128 | tf_op jit(solution)/shard_map/reduce_scatter | solution.py:310
  728.2 109.6 %copy-start.8 = (f32[1,128,2048]{2,1,0:T(8,128)S(1)}, f32[1,128,2048]{2,1,0:T(8,128)}, u32[]{:S(2)}) copy-start(f32[1,128,2048]{2,1,0:T(8,128)} %reduce-scatter.16.cloned.1.call-done) | copy-start | bytes 3145732
  728.2 109.6 %copy-start.13 = (bf16[1,128,2048]{2,1,0:T(8,128)(2,1)S(1)}, bf16[1,128,2048]{2,1,0:T(8,128)(2,1)}, u32[]{:S(2)}) copy-start(bf16[1,128,2048]{2,1,0:T(8,128)(2,1)} %param.16) | copy-start | bytes 1572868
  728.3 109.6 %copy-start.3 = (f32[1,128,2048]{2,1,0:T(8,128)S(1)}, f32[1,128,2048]{2,1,0:T(8,128)}, u32[]{:S(2)}) copy-start(f32[1,128,2048]{2,1,0:T(8,128)} %copy-done.2) | copy-start | bytes 3145732
  (27 other events, 284.4 us)
Sparse Core Ops, SparseCore 0:
  26.2 47.0 all-gather.10
  75.1 26.5 all-gather.12
  103.7 27.8 all-gather.14
  145.1 76.7 reduce-scatter.11
  223.8 43.7 all-gather.20
  269.7 45.9 all-gather.16
  317.7 42.0 all-gather.18
  361.8 43.3 all-gather.22
  426.9 76.7 reduce-scatter.15
  647.3 26.8 reduce-scatter.17
  681.3 76.7 reduce-scatter.19
  760.3 77.4 reduce-scatter.13
  841.9 36.5 reduce-scatter.23
  882.6 51.3 reduce-scatter.25
  937.8 51.2 reduce-scatter.21
  993.4 86.7 reduce-scatter.27
  1084.6 86.7 reduce-scatter.29
  1175.7 86.7 reduce-scatter.31
